TPU v7x, 256 devices: a whole 4x4x8 slice. The times are simulated.
256 devices in a mesh: dp: 8 (over z), fsdp: 16 (over x, y), tensor: 2 (over core).
Axes of the slice: x: 4, y: 4, z: 8, core: 2. Of those that a mesh axis runs over, the one named last changes fastest.
Arguments:
- tokens: bfloat16 [32768, 2048], P('fsdp'), may hold values from -6 to 6
- segment_ids: int32 [32768], P('fsdp'), may hold values from 0 to 127, never falling along the last dimension, each value on 1 to 512 neighbouring positions
- row_order: int32 [32768], P('fsdp'), may hold values from 0 to 2047, as said below
- row_counts: int32 [16], replicated, may hold values from 0 to 1280, as said below
- first_gain: float32 [2048], replicated, may hold values from 0.25 to 1.75
- second_gain: float32 [2048], replicated, may hold values from 0.25 to 1.75
- query_weight: bfloat16 [2048, 2048], P('fsdp', ('dp', 'tensor')), may hold values from -0.110485435 to 0.110485435
- key_weight: bfloat16 [2048, 2048], P('fsdp', ('dp', 'tensor')), may hold values from -4.4636116 to 4.4636116
- value_weight: bfloat16 [2048, 2048], P('fsdp', ('dp', 'tensor')), may hold values from -0.125 to 0.125
- output_weight: bfloat16 [2048, 2048], P(('dp', 'tensor'), 'fsdp'), may hold values from -0.125 to 0.125
- gate_weight: bfloat16 [2048, 8192], P('fsdp', ('dp', 'tensor')), may hold values from -0.125 to 0.125
- up_weight: bfloat16 [2048, 8192], P('fsdp', ('dp', 'tensor')), may hold values from -0.125 to 0.125
- down_weight: bfloat16 [8192, 2048], P(('dp', 'tensor'), 'fsdp'), may hold values from -0.0625 to 0.0625
Outputs:
- recursed: bfloat16 [32768, 2048], P('fsdp', ('dp', 'tensor'))
Inputs may be any that keep to these rules, and one draw needn't show every extreme that they name: `row_counts`: each entry is a multiple of 128, the entries sum to 16384, and the largest entry is exactly 1280. `row_order`: each shard's block of 2048 entries is a permutation of 0 to 2047.
All inputs are finite; a program needn't handle non-finite values.
Results may differ from a plain program's by a relative error of at most 0.015.
Values may be sent and summed in bfloat16 or wider, within the bound.
A program may use at most 128 MiB of HBM per device.

v0:
```python
import math
import jax
import jax.numpy as jnp
from jax import lax
from jax.sharding import PartitionSpec as P

TILE = 128


def rms_scale(row_data, gain_row):
    floats = row_data.astype(jnp.float32)
    inverse = lax.rsqrt(jnp.mean(floats * floats, axis=-1, keepdims=True) + 1e-05)
    return (floats * inverse * gain_row).astype(jnp.bfloat16)


def block_attention(queries, key_rows, value_rows, segments):
    row_total = queries.shape[0]
    block_len = math.gcd(row_total, 512)
    score_scale = 1.0 / math.sqrt(queries.shape[1])
    positions = jnp.arange(row_total, dtype=jnp.int32)

    def one_block(block_id):
        offset = block_id * block_len
        block_rows = lax.dynamic_slice_in_dim(queries, offset, block_len, 0)
        block_segs = lax.dynamic_slice_in_dim(segments, offset, block_len, 0)
        block_pos = offset + jnp.arange(block_len, dtype=jnp.int32)
        scores = (
            lax.dot_general(
                block_rows, key_rows, (((1,), (1,)), ((), ())), preferred_element_type=jnp.float32
            )
            * score_scale
        )
        allowed = (block_segs[:, None] == segments[None, :]) & (
            positions[None, :] <= block_pos[:, None]
        )
        scores = jnp.where(allowed, scores, -1e30)
        peak = jnp.max(scores, axis=-1, keepdims=True)
        expo = jnp.exp(scores - peak)
        probs = (expo / jnp.sum(expo, axis=-1, keepdims=True)).astype(jnp.bfloat16)
        return jnp.dot(probs, value_rows, preferred_element_type=jnp.float32).astype(jnp.bfloat16)

    outputs = lax.map(one_block, jnp.arange(row_total // block_len, dtype=jnp.int32))
    return outputs.reshape(row_total, queries.shape[1])


def feed_forward(ordered_cols, second_gain, gate_weight, up_weight, down_weight):
    full_rows = lax.all_gather(ordered_cols, ("dp", "tensor"), axis=1, tiled=True)
    normed = rms_scale(full_rows, second_gain)
    gate = jnp.dot(
        normed,
        lax.all_gather(gate_weight, "fsdp", axis=0, tiled=True),
        preferred_element_type=jnp.float32,
    )
    upward = jnp.dot(
        normed,
        lax.all_gather(up_weight, "fsdp", axis=0, tiled=True),
        preferred_element_type=jnp.float32,
    )
    hidden = (jax.nn.silu(gate) * upward).astype(jnp.bfloat16)
    terms = jnp.dot(
        hidden,
        lax.all_gather(down_weight, "fsdp", axis=1, tiled=True),
        preferred_element_type=jnp.float32,
    )
    return lax.psum_scatter(
        terms.astype(jnp.bfloat16), ("dp", "tensor"), scatter_dimension=1, tiled=True
    ).astype(jnp.float32)


def body(
    tokens,
    segment_ids,
    row_order,
    row_counts,
    first_gain,
    second_gain,
    query_weight,
    key_weight,
    value_weight,
    output_weight,
    gate_weight,
    up_weight,
    down_weight,
):
    normed = rms_scale(tokens, first_gain)
    weight_pieces = (
        lax.all_gather(query_weight, "fsdp", axis=0, tiled=True),
        lax.all_gather(key_weight, "fsdp", axis=0, tiled=True),
        lax.all_gather(value_weight, "fsdp", axis=0, tiled=True),
    )
    queries, key_rows, value_rows = tuple(
        (
            jnp.dot(normed, weight_piece, preferred_element_type=jnp.float32)
            for weight_piece in weight_pieces
        )
    )
    attended = block_attention(
        queries.astype(jnp.bfloat16),
        key_rows.astype(jnp.bfloat16),
        value_rows.astype(jnp.bfloat16),
        segment_ids,
    )
    head_terms = jnp.dot(
        attended,
        lax.all_gather(output_weight, "fsdp", axis=1, tiled=True),
        preferred_element_type=jnp.float32,
    )
    head_sum = lax.psum_scatter(
        head_terms.astype(jnp.bfloat16), ("dp", "tensor"), scatter_dimension=1, tiled=True
    ).astype(jnp.float32)
    share_cols = head_sum.shape[1]
    member = lax.axis_index(("dp", "tensor"))
    own_cols = lax.dynamic_slice_in_dim(tokens, member * share_cols, share_cols, 1)
    carried = (own_cols.astype(jnp.float32) + head_sum).astype(jnp.bfloat16)
    ordered = jnp.take(carried, row_order, axis=0)
    row_total = tokens.shape[0]
    live_count = lax.dynamic_index_in_dim(row_counts, lax.axis_index("fsdp"), 0, keepdims=False)
    is_live = jnp.arange(row_total, dtype=jnp.int32) < live_count
    own_tiles = row_total // TILE
    cap_rows = (own_tiles // 2 + own_tiles // 8) * TILE
    leading = ordered[:cap_rows]
    summed = feed_forward(leading, second_gain, gate_weight, up_weight, down_weight)
    finished = (leading.astype(jnp.float32) + summed).astype(jnp.bfloat16)
    updated = jnp.concatenate([finished, ordered[cap_rows:]], axis=0)
    token_rows = jnp.take(own_cols, row_order, axis=0)
    mixed = jnp.where(is_live[:, None], updated, token_rows)
    return own_cols.at[row_order].set(mixed)


def solution(mesh):
    in_specs = (
        P("fsdp", None),
        P("fsdp"),
        P("fsdp"),
        P(),
        P(),
        P(),
        P("fsdp", ("dp", "tensor")),
        P("fsdp", ("dp", "tensor")),
        P("fsdp", ("dp", "tensor")),
        P(("dp", "tensor"), "fsdp"),
        P("fsdp", ("dp", "tensor")),
        P("fsdp", ("dp", "tensor")),
        P(("dp", "tensor"), "fsdp"),
    )
    out_specs = P("fsdp", ("dp", "tensor"))
    return jax.shard_map(body, mesh=mesh, in_specs=in_specs, out_specs=out_specs, check_vma=False)
```

profile of v0, /device:TPU:2, one launch (start us, length us, event | category | flops | bytes accessed | tf_op | source)
XLA Modules:
  0.0 566.1 jit_solution(6179705660828530488)
XLA Ops:
  6.5 5.1 fusion.10
  11.7 24.0 %all_gather.26 = bf16[2048,128]{1,0:T(8,128)(2,1)S(1)} all-gather(bf16[128,128]{1,0:T(8,128)(2,1)S(1)} %copy-done.1), channel_id=1, replica_groups=mesh['dp'=8,'fsdp'=16,'tensor'=2] {'fsdp'}, dimensions={0}, use_global_device_ids=true | all-gather | bytes 557056 | tf_op jit(solution)/shard_map/all_gather | solution.py:89
  35.7 22.5 %all_gather.25 = bf16[2048,128]{1,0:T(8,128)(2,1)S(1)} all-gather(bf16[128,128]{1,0:T(8,128)(2,1)S(1)} %copy-done.2), channel_id=1, replica_groups=mesh['dp'=8,'fsdp'=16,'tensor'=2] {'fsdp'}, dimensions={0}, use_global_device_ids=true | all-gather | bytes 557056 | tf_op jit(solution)/shard_map/all_gather | solution.py:88
  58.2 8.6 %fusion.12 = bf16[2048,2048]{1,0:T(8,128)(2,1)} fusion(bf16[2048,2048]{1,0:T(8,128)(2,1)} %param.17, f32[2048]{0:T(1024)S(1)} %copy-done.7, f32[2048]{0:T(1024)S(1)} %add_rsqrt_fusion.1), kind=kLoop, calls=%fused_computation.21 | loop fusion | flops 16777216 | bytes 16793600 | tf_op jit(solution)/shard_map/convert_element_type | solution.py:13
  66.7 5.9 %convolution_convert_fusion.2 = bf16[2048,128]{1,0:T(8,128)(2,1)S(1)} fusion(bf16[2048,2048]{1,0:T(8,128)(2,1)} %fusion.12, bf16[2048,128]{1,0:T(8,128)(2,1)S(1)} %all_gather.26), kind=kOutput, calls=%fused_computation.31 | convolution fusion | flops 1074003968 | bytes 9437184 | tf_op jit(solution)/shard_map/dot_general | solution.py:93
  72.6 2.4 convolution_convert_fusion.3
  75.0 22.8 %all_gather.24 = bf16[2048,128]{1,0:T(8,128)(2,1)S(1)} all-gather(bf16[128,128]{1,0:T(8,128)(2,1)S(1)} %copy-done.3), channel_id=1, replica_groups=mesh['dp'=8,'fsdp'=16,'tensor'=2] {'fsdp'}, dimensions={0}, use_global_device_ids=true | all-gather | bytes 557056 | tf_op jit(solution)/shard_map/all_gather | solution.py:87
  97.8 2.4 convolution_convert_fusion.4
  100.3 17.5 %while.11 = (s32[]{:T(128)}, bf16[4,512,128]{2,1,0:T(8,128)(2,1)S(1)}, s32[4]{0:T(128)S(1)}, s32[2048]{0:T(1024)S(1)}, bf16[2048,128]{1,0:T(8,128)(2,1)S(1)}, /*...) while((s32[]{:T(128)}, ...), condition=%wide.region_4.5_spmd.clone, body=%wide.region_1.4_spmd.clone.sunk | while | flops 548470272 | bytes 13922487 | solution.py:42
  101.6 1.3 fusion.53
  106.0 1.4 fusion.53
  108.1 0.9 fusion.55
  110.4 1.4 fusion.53
  114.7 1.4 fusion.53
  117.8 23.1 %all_gather.27 = bf16[128,2048]{1,0:T(8,128)(2,1)S(1)} all-gather(bf16[128,128]{1,0:T(8,128)(2,1)S(1)} %copy-done.4), channel_id=1, replica_groups=mesh['dp'=8,'fsdp'=16,'tensor'=2] {'fsdp'}, dimensions={1}, use_global_device_ids=true | all-gather | bytes 557056 | tf_op jit(solution)/shard_map/all_gather | solution.py:105
  140.8 5.6 convolution_convert_fusion.1
  146.4 12.3 %copy.14 = bf16[2048,2048]{0,1:T(8,128)(2,1)} copy(bf16[2048,2048]{1,0:T(8,128)(2,1)} %convolution_convert_fusion.1) | data formatting | bytes 16777216
  159.4 71.6 %reduce-scatter.7.cloned.1.call-done = bf16[128,2048]{1,0:T(8,128)(2,1)} async-done(((bf16[2048,2048]{1,0:T(8,128)(2,1)}), bf16[128,2048]{1,0:T(8,128)(2,1)}) %reduce-scatter.7.cloned.1.call-update) | async-done | bytes 524304
  231.0 1.3 copy.15
  232.3 2.0 add_convert_fusion
  234.3 6.2 %gather_fusion = bf16[2048,128]{1,0:T(8,128)(2,1)S(1)} fusion(bf16[2048,128]{1,0:T(8,128)(2,1)S(1)} %get-tuple-element.79, s32[2048]{0:T(1024)S(1)} %get-tuple-element.83), kind=kCustom, calls=%fused_computation.clone | custom fusion | bytes 1056768 | tf_op jit(solution)/shard_map/jit(_take)/gather | solution.py:115
  243.8 49.9 %all-gather.5.cloned.1.call-done = bf16[1280,2048]{1,0:T(8,128)(2,1)} async-done(((bf16[1280,128]{1,0:T(8,128)(2,1)}), bf16[1280,2048]{1,0:T(8,128)(2,1)}) %all-gather.5.cloned.1.call-update) | async-done | bytes 5242896 | tf_op jit(solution)/shard_map/all_gather | solution.py:47
  293.7 3.6 fusion.13
  297.3 47.7 %all-gather.7.cloned.1.call-done = bf16[2048,512]{1,0:T(8,128)(2,1)} async-done(((bf16[128,512]{1,0:T(8,128)(2,1)}), bf16[2048,512]{1,0:T(8,128)(2,1)}) %all-gather.7.cloned.1.call-update) | async-done | bytes 2097168 | tf_op jit(solution)/shard_map/all_gather | solution.py:51
  345.0 7.6 %fusion.18 = f32[1280,512]{1,0:T(8,128)} fusion(bf16[2048,512]{1,0:T(8,128)(2,1)} %all-gather.7.cloned.1.call-done, bf16[1280,2048]{1,0:T(8,128)(2,1)} %all-gather.5.cloned.1.call-done, f32[2048]{0:T(1024)S(1)} %copy-done.8, f32[1280]{0:T(1024)S(1)} %add_rsqrt_fusion), kind=kOutput, calls=%fused_computation.34 | convolution fusion | flops 2694840320 | bytes 9974784 | tf_op jit(solution)/shard_map/dot_general | solution.py:49
  352.6 46.1 %all-gather.11.cloned.1.call-done = bf16[512,2048]{1,0:T(8,128)(2,1)} async-done(((bf16[512,128]{1,0:T(8,128)(2,1)}), bf16[512,2048]{1,0:T(8,128)(2,1)}) %all-gather.11.cloned.1.call-update) | async-done | bytes 2097168 | tf_op jit(solution)/shard_map/all_gather | solution.py:62
  398.7 51.6 %all-gather.9.cloned.1.call-done = bf16[2048,512]{1,0:T(8,128)(2,1)} async-done(((bf16[128,512]{1,0:T(8,128)(2,1)}), bf16[2048,512]{1,0:T(8,128)(2,1)}) %all-gather.9.cloned.1.call-update) | async-done | bytes 2097168 | tf_op jit(solution)/shard_map/all_gather | solution.py:56
  450.4 11.2 %convolution_convert_fusion = bf16[1280,2048]{1,0:T(8,128)(2,1)} fusion(bf16[512,2048]{1,0:T(8,128)(2,1)} %all-gather.11.cloned.1.call-done, bf16[2048,512]{1,0:T(8,128)(2,1)} %all-gather.9.cloned.1.call-done, f32[1280,512]{1,0:T(8,128)} %fusion.18, bf16[1280,2048]{1,0:T(8,128)(2,1)} %all-gather.5.cloned.1.call-done, f32[2048]{0:T(1024)S(1)} %copy-done.8, ...), kind=kOutput, calls=%fused_computation.27 | convolution fusion | flops 5385748480 | bytes 17314816 | tf_op jit(solution)/shard_map/dot_general | solution.py:60
  461.6 7.9 %copy.16 = bf16[1280,2048]{0,1:T(8,128)(2,1)} copy(bf16[1280,2048]{1,0:T(8,128)(2,1)} %convolution_convert_fusion) | data formatting | bytes 10485760
  471.3 63.3 %reduce-scatter.9.cloned.1.call-done = bf16[128,1280]{1,0:T(8,128)(2,1)} async-done(((bf16[2048,1280]{1,0:T(8,128)(2,1)}), bf16[128,1280]{1,0:T(8,128)(2,1)}) %reduce-scatter.9.cloned.1.call-update) | async-done | bytes 327696
  534.6 1.2 copy.17
  535.9 23.4 %scatter_custom_fusion = bf16[2048,128]{1,0:T(8,128)(2,1)} fusion(bf16[2048,128]{1,0:T(8,128)(2,1)} %get-tuple-element.80, s32[2048]{0:T(1024)S(1)} %get-tuple-element.84, bf16[768,128]{1,0:T(8,128)(2,1)S(1)} %slice.13, bf16[]{:T(256)} %constant.75, bf16[1280,128]{1,0:T(8,128)(2,1)S(1)} %add_convert_fusion.1, pred[2048]{0:T(1024)(128)(4,1)S(1)} %compare_and_fusion, ...), kind=kCustom, calls=%fused_computation.39 | custom fusion | flops 1572864 | bytes 1585156 | tf_op jit(solution)/shard_map/scatter | solution.py:127
  (63 shorter events, 14.3 us)
Async XLA Ops:
  6.5 5.1 copy-start.1
  6.5 29.1 %copy-start.2 = (bf16[128,128]{1,0:T(8,128)(2,1)S(1)}, bf16[128,128]{1,0:T(8,128)(2,1)}, u32[]{:S(2)}) copy-start(bf16[128,128]{1,0:T(8,128)(2,1)} %param.24) | copy-start | bytes 98308
  6.5 51.6 %copy-start.7 = (f32[2048]{0:T(1024)S(1)}, f32[2048]{0:T(1024)}, u32[]{:S(2)}) copy-start(f32[2048]{0:T(1024)} %param.21) | copy-start | bytes 24580
  6.5 224.5 %reduce-scatter.7.cloned.1.call-start = ((), (), s32[]{:S(2)}) async-start(), calls=%async_computation.6 | async-start | bytes 8912896
  66.7 5.9 %copy-start = (bf16[2048,2048]{1,0:T(8,128)(2,1)S(1)}, bf16[2048,2048]{1,0:T(8,128)(2,1)}, u32[]{:S(2)}) copy-start(bf16[2048,2048]{1,0:T(8,128)(2,1)} %fusion.12) | copy-start | bytes 25165828
  72.6 2.4 copy-start.3
  97.8 2.4 copy-start.6
  100.3 17.5 %copy-start.4 = (bf16[128,128]{1,0:T(8,128)(2,1)S(1)}, bf16[128,128]{1,0:T(8,128)(2,1)}, u32[]{:S(2)}) copy-start(bf16[128,128]{1,0:T(8,128)(2,1)} %param.26) | copy-start | bytes 98308
  158.7 0.7 copy-start.5
  158.7 135.0 %all-gather.5.cloned.1.call-start = ((), (), s32[]{:S(2)}) async-start(), calls=%async_computation.2 | async-start | bytes 5570560 | tf_op jit(solution)/shard_map/all_gather | solution.py:47
  234.3 110.7 %copy-start.8 = (f32[2048]{0:T(1024)S(1)}, f32[2048]{0:T(1024)}, u32[]{:S(2)}) copy-start(f32[2048]{0:T(1024)} %param.22) | copy-start | bytes 24580
  241.6 103.4 %all-gather.7.cloned.1.call-start = ((), (), s32[]{:S(2)}) async-start(), calls=%async_computation.3 | async-start | bytes 2228224 | tf_op jit(solution)/shard_map/all_gather | solution.py:51
  242.3 156.4 %all-gather.11.cloned.1.call-start = ((), (), s32[]{:S(2)}) async-start(), calls=%async_computation.5 | async-start | bytes 2228224 | tf_op jit(solution)/shard_map/all_gather | solution.py:62
  242.9 207.5 %all-gather.9.cloned.1.call-start = ((), (), s32[]{:S(2)}) async-start(), calls=%async_computation.4 | async-start | bytes 2228224 | tf_op jit(solution)/shard_map/all_gather | solution.py:56
  243.5 291.1 %reduce-scatter.9.cloned.1.call-start = ((), (), s32[]{:S(2)}) async-start(), calls=%async_computation.7 | async-start | bytes 5570560
  469.5 0.7 copy-start.9
Sparse Core Ops, SparseCore 0:
  158.8 72.1 reduce-scatter.6
  241.7 51.9 all-gather.4
  296.1 48.8 all-gather.6
  347.3 51.4 all-gather.10
  401.0 49.3 all-gather.8
  469.6 64.9 reduce-scatter.8
where the time goes:
time: 567 us; the launch traced here: 566 us
  waiting for transfers between devices  332 us (59%)
  blocking collectives  92.4 us (16%)
  other arithmetic  46.5 us (8%)
  matrix products  44.3 us (8%)
  local copies, waits for them, and re-layouts  34.2 us (6%)
  between operations  13.7 us (2%)
    unnamed x8, waiting for transfers between devices  137 us
    all_gather x1, waiting for transfers between devices, feed_forward(): lax.all_gather(up_weight, 'fsdp', axis=0, tiled=True)  51.6 us
    all_gather x1, waiting for transfers between devices, feed_forward(): lax.all_gather(ordered_cols, ('dp', 'tensor'), axis=1, tiled=True)  49.9 us
    all_gather x1, waiting for transfers between devices, feed_forward(): lax.all_gather(gate_weight, 'fsdp', axis=0, tiled=True)  47.7 us
    all_gather x1, waiting for transfers between devices, feed_forward(): lax.all_gather(down_weight, 'fsdp', axis=1, tiled=True)  46.1 us
    all_gather x1, blocking collectives, body(): lax.all_gather(value_weight, 'fsdp', axis=0, tiled=True)  24 us
    unnamed x24, local copies, waits for them, and re-layouts  23.9 us
    scatter x1, other arithmetic, body(): return own_cols.at[row_order].set(mixed)  23.4 us
  transfers between devices with their start and end apart: 6, of which 6 were waited for; matrix products, arithmetic and copies ran while one was open for 2% of the time, Pallas kernels for 0%

commit v1 on v0

--- a/solution.py
+++ b/solution.py
@@ -59,7 +59,9 @@
     hidden = (jax.nn.silu(gate) * upward).astype(jnp.bfloat16)
     terms = jnp.dot(
         hidden,
-        lax.all_gather(down_weight, "fsdp", axis=1, tiled=True),
+        jnp.concatenate(
+            lax.all_to_all(jnp.stack([down_weight] * lax.axis_size("fsdp")), "fsdp", 0, 0), axis=1
+        ),
         preferred_element_type=jnp.float32,
     )
     return lax.psum_scatter(

time: 567 us -> 512 us (0.903)
  waiting for transfers between devices: 332 us -> 268 us
  starting transfers between devices: 0.42 us -> 7.99 us
    all_gather x1 -> x0, waiting for transfers between devices: 46.1 us -> none  [feed_forward(): lax.all_gather(down_weight, 'fsdp', axis=1, tiled=True)]
    all_gather x1, waiting for transfers between devices: 49.9 us -> 40.7 us  [feed_forward(): lax.all_gather(ordered_cols, ('dp', 'tensor'), axis=1, tiled=True)]
    all_gather x1, waiting for transfers between devices: 51.6 us -> 44 us  [feed_forward(): lax.all_gather(up_weight, 'fsdp', axis=0, tiled=True)]
    all_to_all x0 -> x1, starting transfers between devices: none -> 7.61 us  [feed_forward(): lax.all_to_all(jnp.stack([down_weight] * lax.axis_size('fsdp')), 'fsdp',...]
    unnamed x8 -> x7, waiting for transfers between devices: 137 us -> 136 us
    unnamed x24 -> x27, local copies, waits for them, and re-layouts: 23.9 us -> 24 us
  transfers between devices with their start and end apart: 6 -> 6, of which waited for: 6 -> 5; matrix products, arithmetic and copies ran while one was open for 2% -> 3% of each run, Pallas kernels for 0% -> 0%
where the time goes in v1:
time: 512 us; the launch traced here: 511 us
  waiting for transfers between devices  268 us (52%)
  blocking collectives  92.4 us (18%)
  other arithmetic  46.5 us (9%)
  matrix products  43.7 us (9%)
  local copies, waits for them, and re-layouts  35.9 us (7%)
  between operations  13.3 us (3%)
  starting transfers between devices  7.99 us (2%)
    unnamed x7, waiting for transfers between devices  136 us
    all_gather x1, waiting for transfers between devices, feed_forward(): lax.all_gather(gate_weight, 'fsdp', axis=0, tiled=True)  47.7 us
    all_gather x1, waiting for transfers between devices, feed_forward(): lax.all_gather(up_weight, 'fsdp', axis=0, tiled=True)  44 us
    all_gather x1, waiting for transfers between devices, feed_forward(): lax.all_gather(ordered_cols, ('dp', 'tensor'), axis=1, tiled=True)  40.7 us
    unnamed x27, local copies, waits for them, and re-layouts  24 us
    all_gather x1, blocking collectives, body(): lax.all_gather(value_weight, 'fsdp', axis=0, tiled=True)  24 us
    scatter x1, other arithmetic, body(): return own_cols.at[row_order].set(mixed)  23.4 us
    all_gather x1, blocking collectives, body(): lax.all_gather(output_weight, 'fsdp', axis=1, tiled=True)  23.1 us
  transfers between devices with their start and end apart: 6, of which 5 were waited for; matrix products, arithmetic and copies ran while one was open for 3% of the time, Pallas kernels for 0%

profile of v1, /device:TPU:2, one launch (start us, length us, event | category | flops | bytes accessed | tf_op | source)
XLA Modules:
  0.0 510.8 jit_solution(6873906428694653952)
XLA Ops:
  6.5 5.1 %fusion.10 = f32[2048]{0:T(1024)S(1)} fusion(bf16[2048,2048]{1,0:T(8,128)(2,1)} %param.17), kind=kLoop, calls=%fused_computation.19 | loop fusion | flops 12580864 | bytes 8396800 | tf_op jit(solution)/shard_map/reduce_sum | solution.py:12
  11.7 24.0 %all_gather.23 = bf16[2048,128]{1,0:T(8,128)(2,1)S(1)} all-gather(bf16[128,128]{1,0:T(8,128)(2,1)S(1)} %copy-done.2), channel_id=1, replica_groups=mesh['dp'=8,'fsdp'=16,'tensor'=2] {'fsdp'}, dimensions={0}, use_global_device_ids=true | all-gather | bytes 557056 | tf_op jit(solution)/shard_map/all_gather | solution.py:91
  35.7 22.5 %all_gather.22 = bf16[2048,128]{1,0:T(8,128)(2,1)S(1)} all-gather(bf16[128,128]{1,0:T(8,128)(2,1)S(1)} %copy-done.3), channel_id=1, replica_groups=mesh['dp'=8,'fsdp'=16,'tensor'=2] {'fsdp'}, dimensions={0}, use_global_device_ids=true | all-gather | bytes 557056 | tf_op jit(solution)/shard_map/all_gather | solution.py:90
  58.2 8.6 %fusion.12 = bf16[2048,2048]{1,0:T(8,128)(2,1)} fusion(bf16[2048,2048]{1,0:T(8,128)(2,1)} %param.17, f32[2048]{0:T(1024)S(1)} %copy-done.8, f32[2048]{0:T(1024)S(1)} %add_rsqrt_fusion.1), kind=kLoop, calls=%fused_computation.21 | loop fusion | flops 16777216 | bytes 16793600 | tf_op jit(solution)/shard_map/convert_element_type | solution.py:13
  66.7 5.9 %convolution_convert_fusion.2 = bf16[2048,128]{1,0:T(8,128)(2,1)S(1)} fusion(bf16[2048,2048]{1,0:T(8,128)(2,1)} %fusion.12, bf16[2048,128]{1,0:T(8,128)(2,1)S(1)} %all_gather.23), kind=kOutput, calls=%fused_computation.31 | convolution fusion | flops 1074003968 | bytes 9437184 | tf_op jit(solution)/shard_map/dot_general | solution.py:95
  72.6 2.4 convolution_convert_fusion.3
  75.0 22.8 %all_gather.21 = bf16[2048,128]{1,0:T(8,128)(2,1)S(1)} all-gather(bf16[128,128]{1,0:T(8,128)(2,1)S(1)} %copy-done.4), channel_id=1, replica_groups=mesh['dp'=8,'fsdp'=16,'tensor'=2] {'fsdp'}, dimensions={0}, use_global_device_ids=true | all-gather | bytes 557056 | tf_op jit(solution)/shard_map/all_gather | solution.py:89
  97.8 2.4 convolution_convert_fusion.4
  100.3 17.5 %while.11 = (s32[]{:T(128)}, bf16[4,512,128]{2,1,0:T(8,128)(2,1)S(1)}, s32[4]{0:T(128)S(1)}, s32[2048]{0:T(1024)S(1)}, bf16[2048,128]{1,0:T(8,128)(2,1)S(1)}, /*...) while((s32[]{:T(128)}, ...), condition=%wide.region_4.5_spmd.clone, body=%wide.region_1.4_spmd.clone.sunk | while | flops 548470272 | bytes 13922487 | solution.py:42
  101.6 1.3 fusion.53
  106.0 1.4 fusion.53
  110.4 1.4 fusion.53
  114.7 1.4 fusion.53
  117.8 23.1 %all_gather.24 = bf16[128,2048]{1,0:T(8,128)(2,1)S(1)} all-gather(bf16[128,128]{1,0:T(8,128)(2,1)S(1)} %copy-done.5), channel_id=1, replica_groups=mesh['dp'=8,'fsdp'=16,'tensor'=2] {'fsdp'}, dimensions={1}, use_global_device_ids=true | all-gather | bytes 557056 | tf_op jit(solution)/shard_map/all_gather | solution.py:107
  140.8 5.6 %convolution_convert_fusion.1 = bf16[2048,2048]{1,0:T(8,128)(2,1)} fusion(bf16[2048,128]{1,0:T(8,128)(2,1)S(1)} %bitcast.38, bf16[128,2048]{1,0:T(8,128)(2,1)S(1)} %all_gather.24), kind=kOutput, calls=%fused_computation.28 | convolution fusion | flops 1077936128 | bytes 9437184 | tf_op jit(solution)/shard_map/dot_general | solution.py:105
  146.4 12.3 %copy.16 = bf16[2048,2048]{0,1:T(8,128)(2,1)} copy(bf16[2048,2048]{1,0:T(8,128)(2,1)} %convolution_convert_fusion.1) | data formatting | bytes 16777216
  159.4 71.6 %reduce-scatter.7.cloned.1.call-done = bf16[128,2048]{1,0:T(8,128)(2,1)} async-done(((bf16[2048,2048]{1,0:T(8,128)(2,1)}), bf16[128,2048]{1,0:T(8,128)(2,1)}) %reduce-scatter.7.cloned.1.call-update) | async-done | bytes 524304
  231.0 1.3 copy.17
  232.3 2.0 add_convert_fusion
  234.3 6.2 %gather_fusion = bf16[2048,128]{1,0:T(8,128)(2,1)S(1)} fusion(bf16[2048,128]{1,0:T(8,128)(2,1)S(1)} %get-tuple-element.79, s32[2048]{0:T(1024)S(1)} %get-tuple-element.83), kind=kCustom, calls=%fused_computation.clone | custom fusion | bytes 1056768 | tf_op jit(solution)/shard_map/jit(_take)/gather | solution.py:117
  243.1 1.6 stack.2
  244.7 7.6 %all-to-all-start = ((bf16[16,512,128]{1,2,0:T(8,128)(2,1)}), bf16[16,512,128]{1,2,0:T(8,128)(2,1)S(1)}, u32[]{:S(2)}, u32[]{:S(2)}) async-start(bf16[16,512,128]{1,2,0:T(8,128)(2,1)} %stack.2), calls=%async_computation | async-start | bytes 4194304 | tf_op jit(solution)/shard_map/all_to_all | solution.py:63
  252.5 40.7 %all-gather.4.cloned.1.call-done = bf16[1280,2048]{1,0:T(8,128)(2,1)} async-done(((bf16[1280,128]{1,0:T(8,128)(2,1)}), bf16[1280,2048]{1,0:T(8,128)(2,1)}) %all-gather.4.cloned.1.call-update) | async-done | bytes 5242896 | tf_op jit(solution)/shard_map/all_gather | solution.py:47
  293.3 3.6 fusion.13
  296.9 47.7 %all-gather.6.cloned.1.call-done = bf16[2048,512]{1,0:T(8,128)(2,1)} async-done(((bf16[128,512]{1,0:T(8,128)(2,1)}), bf16[2048,512]{1,0:T(8,128)(2,1)}) %all-gather.6.cloned.1.call-update) | async-done | bytes 2097168 | tf_op jit(solution)/shard_map/all_gather | solution.py:51
  344.5 7.6 %fusion.18 = f32[1280,512]{1,0:T(8,128)} fusion(bf16[2048,512]{1,0:T(8,128)(2,1)} %all-gather.6.cloned.1.call-done, bf16[1280,2048]{1,0:T(8,128)(2,1)} %all-gather.4.cloned.1.call-done, f32[2048]{0:T(1024)S(1)} %copy-done.9, f32[1280]{0:T(1024)S(1)} %add_rsqrt_fusion), kind=kOutput, calls=%fused_computation.34 | convolution fusion | flops 2694840320 | bytes 9974784 | tf_op jit(solution)/shard_map/dot_general | solution.py:49
  352.2 44.0 %all-gather.8.cloned.1.call-done = bf16[2048,512]{1,0:T(8,128)(2,1)} async-done(((bf16[128,512]{1,0:T(8,128)(2,1)}), bf16[2048,512]{1,0:T(8,128)(2,1)}) %all-gather.8.cloned.1.call-update) | async-done | bytes 2097168 | tf_op jit(solution)/shard_map/all_gather | solution.py:56
  396.2 10.6 %convolution_convert_fusion = bf16[1280,2048]{1,0:T(8,128)(2,1)} fusion(bf16[512,2048]{0,1:T(8,128)(2,1)S(1)} %bitcast.37, bf16[2048,512]{1,0:T(8,128)(2,1)} %all-gather.8.cloned.1.call-done, f32[1280,512]{1,0:T(8,128)} %fusion.18, bf16[1280,2048]{1,0:T(8,128)(2,1)} %all-gather.4.cloned.1.call-done, f32[2048]{0:T(1024)S(1)} %copy-done.9, ...), kind=kOutput, calls=%fused_computation.27 | convolution fusion | flops 5385748480 | bytes 17314816 | tf_op jit(solution)/shard_map/dot_general | solution.py:60
  406.8 7.9 %copy.18 = bf16[1280,2048]{0,1:T(8,128)(2,1)} copy(bf16[1280,2048]{1,0:T(8,128)(2,1)} %convolution_convert_fusion) | data formatting | bytes 10485760
  416.5 63.2 %reduce-scatter.9.cloned.1.call-done = bf16[128,1280]{1,0:T(8,128)(2,1)} async-done(((bf16[2048,1280]{1,0:T(8,128)(2,1)}), bf16[128,1280]{1,0:T(8,128)(2,1)}) %reduce-scatter.9.cloned.1.call-update) | async-done | bytes 327696
  479.6 1.2 copy.19
  480.9 23.4 %scatter_custom_fusion = bf16[2048,128]{1,0:T(8,128)(2,1)} fusion(bf16[2048,128]{1,0:T(8,128)(2,1)} %get-tuple-element.80, s32[2048]{0:T(1024)S(1)} %get-tuple-element.84, bf16[768,128]{1,0:T(8,128)(2,1)S(1)} %slice.13, bf16[]{:T(256)} %constant.75, bf16[1280,128]{1,0:T(8,128)(2,1)S(1)} %add_convert_fusion.1, pred[2048]{0:T(1024)(128)(4,1)S(1)} %compare_and_fusion, ...), kind=kCustom, calls=%fused_computation.39 | custom fusion | flops 1572864 | bytes 1585156 | tf_op jit(solution)/shard_map/scatter | solution.py:129
  (66 shorter events, 14.8 us)
Async XLA Ops:
  6.5 5.1 %copy-start.2 = (bf16[128,128]{1,0:T(8,128)(2,1)S(1)}, bf16[128,128]{1,0:T(8,128)(2,1)}, u32[]{:S(2)}) copy-start(bf16[128,128]{1,0:T(8,128)(2,1)} %param.25) | copy-start | bytes 98308
  6.5 29.1 %copy-start.3 = (bf16[128,128]{1,0:T(8,128)(2,1)S(1)}, bf16[128,128]{1,0:T(8,128)(2,1)}, u32[]{:S(2)}) copy-start(bf16[128,128]{1,0:T(8,128)(2,1)} %param.24) | copy-start | bytes 98308
  6.5 51.6 %copy-start.8 = (f32[2048]{0:T(1024)S(1)}, f32[2048]{0:T(1024)}, u32[]{:S(2)}) copy-start(f32[2048]{0:T(1024)} %param.21) | copy-start | bytes 24580
  6.5 224.5 %reduce-scatter.7.cloned.1.call-start = ((), (), s32[]{:S(2)}) async-start(), calls=%async_computation.6 | async-start | bytes 8912896
  66.7 5.9 %copy-start = (bf16[2048,2048]{1,0:T(8,128)(2,1)S(1)}, bf16[2048,2048]{1,0:T(8,128)(2,1)}, u32[]{:S(2)}) copy-start(bf16[2048,2048]{1,0:T(8,128)(2,1)} %fusion.12) | copy-start | bytes 25165828
  72.6 2.4 copy-start.4
  97.8 2.4 copy-start.7
  100.3 17.5 %copy-start.5 = (bf16[128,128]{1,0:T(8,128)(2,1)S(1)}, bf16[128,128]{1,0:T(8,128)(2,1)}, u32[]{:S(2)}) copy-start(bf16[128,128]{1,0:T(8,128)(2,1)} %param.26) | copy-start | bytes 98308
  158.7 0.7 copy-start.6
  158.7 84.2 %copy-start.1 = (bf16[512,128]{1,0:T(8,128)(2,1)S(1)}, bf16[512,128]{1,0:T(8,128)(2,1)}, u32[]{:S(2)}) copy-start(bf16[512,128]{1,0:T(8,128)(2,1)} %param.29) | copy-start | bytes 393220
  158.7 134.5 %all-gather.4.cloned.1.call-start = ((), (), s32[]{:S(2)}) async-start(), calls=%async_computation.3 | async-start | bytes 5570560 | tf_op jit(solution)/shard_map/all_gather | solution.py:47
  241.6 102.9 %all-gather.6.cloned.1.call-start = ((), (), s32[]{:S(2)}) async-start(), calls=%async_computation.4 | async-start | bytes 2228224 | tf_op jit(solution)/shard_map/all_gather | solution.py:51
  242.4 153.8 %all-gather.8.cloned.1.call-start = ((), (), s32[]{:S(2)}) async-start(), calls=%async_computation.5 | async-start | bytes 2228224 | tf_op jit(solution)/shard_map/all_gather | solution.py:56
  244.7 99.9 %copy-start.9 = (f32[2048]{0:T(1024)S(1)}, f32[2048]{0:T(1024)}, u32[]{:S(2)}) copy-start(f32[2048]{0:T(1024)} %param.22) | copy-start | bytes 24580
  244.7 107.5 %all-to-all-start = ((bf16[16,512,128]{1,2,0:T(8,128)(2,1)}), bf16[16,512,128]{1,2,0:T(8,128)(2,1)S(1)}, u32[]{:S(2)}, u32[]{:S(2)}) async-start(bf16[16,512,128]{1,2,0:T(8,128)(2,1)} %stack.2), calls=%async_computation | async-start | bytes 4194304 | tf_op jit(solution)/shard_map/all_to_all | solution.py:63
  252.3 227.4 %reduce-scatter.9.cloned.1.call-start = ((), (), s32[]{:S(2)}) async-start(), calls=%async_computation.7 | async-start | bytes 5570560
  414.6 0.7 copy-start.10
Sparse Core Ops, SparseCore 0:
  158.8 72.1 reduce-scatter.6
  241.7 51.4 all-gather.3
  295.7 48.7 all-gather.5
  346.8 49.3 all-gather.7
  414.8 64.8 reduce-scatter.8
